TPU v7x, 32 devices: a whole 2x2x4 slice. The times are simulated.
32 devices in a mesh: group: 2 (over x), reader: 16 (over z, y, core).
Axes of the slice: x: 2, y: 2, z: 4, core: 2. Of those that a mesh axis runs over, the one named last changes fastest.
Arguments:
- answer_lengths: int32 [64], P('group'), parts along dimension 0, may hold values from 1 to 256, 4096 in all
- mixer_input: bfloat16 [8192, 4096], P(('group', 'reader')), parts along dimension 0, may hold values from -6 to 6
- gate_input: bfloat16 [8192, 4096], P(('group', 'reader')), parts along dimension 0, may hold values from -6 to 6
- state_write: bfloat16 [8192, 512], P(('group', 'reader')), parts along dimension 0, may hold values from -6 to 6
- state_read: bfloat16 [8192, 512], P(('group', 'reader')), parts along dimension 0, may hold values from -0.5 to 0.5
- step_raw: float32 [8192, 64], P(('group', 'reader')), parts along dimension 0, may hold values from -4 to 50
- decay_rate: float32 [64], replicated, may hold values from 0.006 to 0.15
- skip_gain: float32 [64], replicated, may hold values from 0.5 to 2
- norm_gain: float32 [4096], replicated, may hold values from 0.1 to 1.9
- prompt_state: float32 [8192, 128], P(('group', 'reader')), parts along dimension 0, may hold values from -24 to 24
- queries: bfloat16 [8192, 2048], P(('group', 'reader')), parts along dimension 0, may hold values from -160 to 160
- answer_keys: bfloat16 [8192, 512], P(('group', 'reader')), parts along dimension 0, may hold values from -6 to 6
- answer_values: bfloat16 [8192, 512], P(('group', 'reader')), parts along dimension 0, may hold values from -48 to 48
- prompt_keys: bfloat16 [256, 512], P(('group', 'reader')), parts along dimension 0, may hold values from -4 to 4
- prompt_values: bfloat16 [256, 512], P(('group', 'reader')), parts along dimension 0, may hold values from -48 to 48
Outputs:
- mixer_out: bfloat16 [8192, 4096], P(('group', 'reader')), parts along dimension 0
- attention_out: bfloat16 [8192, 2048], P(('group', 'reader')), parts along dimension 0
There are 2 independent parts, one for each index of `group`. A program takes and returns all parts, laid end to end along the dimension named above; an argument that names none is the same for every part. Nothing has to cross between parts.
Inputs may be any that keep to these rules, and one draw needn't show every extreme that they name: `answer_lengths`: the answers fill the 4096 tokens in order, back to back; the longest has exactly 256 tokens.
All inputs are finite; a program needn't handle non-finite values.
Results may differ from a plain program's by a relative error of at most 0.0047.
Values may be sent and summed in bfloat16 or wider, within the bound.
A program may use at most 128 MiB of HBM per device.

v0:
```python
import functools
import math

import jax
import jax.numpy as jnp
from jax import lax
from jax.experimental import pallas as pl
from jax.experimental.pallas import tpu as pltpu
from jax.sharding import PartitionSpec as P

HD = 128
F32 = jnp.float32
BF16 = jnp.bfloat16
MESH = pl.DeviceIdType.MESH
VMEM_LIMIT = 60 * 1024 * 1024


def iota(shape, axis):
    return lax.broadcasted_iota(jnp.int32, shape, axis)


def nt(a, b):
    return lax.dot_general(a, b, (((1,), (1,)), ((), ())), preferred_element_type=F32)


def starts_of_column(lengths_row, first, rows):
    n = lengths_row.shape[1]
    wide = jnp.broadcast_to(lengths_row.astype(F32), (8, n)).astype(BF16)
    ahead = (iota((n, n), 0) < iota((n, n), 1)).astype(F32).astype(BF16)
    starts = jnp.dot(wide, ahead, preferred_element_type=F32)[0:1, :]
    place = (iota((rows, n), 0) + first).astype(F32)
    return jnp.max(jnp.where(starts <= place, starts, -1.0), axis=1, keepdims=True)


def starts_of_row(lengths_row, first, columns):
    n = lengths_row.shape[1]
    wide = jnp.broadcast_to(lengths_row.astype(F32), (8, n)).astype(BF16)
    ahead = (iota((n, n), 1) < iota((n, n), 0)).astype(F32).astype(BF16)
    starts = nt(ahead, wide)[:, 0:1]
    place = (iota((n, columns), 1) + first).astype(F32)
    return jnp.max(jnp.where(starts <= place, starts, -1.0), axis=0, keepdims=True)


def column_of(value, index):
    lanes = iota(value.shape, 1)
    return jnp.sum(jnp.where(lanes == index, value, 0.0), axis=1, keepdims=True)


def pair_of(value, index, low):
    return jnp.where(low, column_of(value, index), column_of(value, index + 1))


def mix_kernel(
    readers, bits, groups,
    lengths, x, write, read, raw, rate, skip, prompt, pkeys, pvalues, keys, values,
    y_out, seed_out, pk_out, pv_out, d_prompt, d_state, prior_k, prior_v, prior_state,
    seed_buf, kv_buf, state_buf, tail_buf, tail_in, lo, lo_t, weight, write_t, inner,
    send, recv,
):
    rows = x.shape[0]
    heads = raw.shape[1]
    per_group = heads // groups
    size = write.shape[1] // groups
    pairs = x.shape[1] // 128
    pairs_per_group = pairs // groups
    me = lax.axis_index("reader")
    after = lax.rem(me + 1, readers)
    ahead = lax.rem(me + readers - 1, readers)
    partners = []
    slot = 0
    for step in range(bits):
        unit = 1 << (bits - 1 - step)
        bit = lax.rem(me // unit, 2)
        partners.append(me + unit * (1 - 2 * bit))
        slot = slot + bit * (1 << step)
    barrier = pltpu.get_barrier_semaphore()
    for other in partners + [after, ahead]:
        pl.semaphore_signal(barrier, inc=1, device_id={"reader": other}, device_id_type=MESH)
    seed_buf[slot] = prompt[...].astype(BF16)
    few = pkeys.shape[0]
    kv_buf[slot] = jnp.concatenate([pkeys[...], pvalues[...]], axis=0)
    pl.semaphore_wait(barrier, bits + 2)

    def remote(source, target, index, other):
        return pltpu.make_async_remote_copy(
            src_ref=source, dst_ref=target, send_sem=send.at[index], recv_sem=recv.at[index],
            device_id={"reader": other}, device_id_type=MESH,
        )

    def gather(step):
        count = 1 << step
        base = (slot // count) * count
        block = pl.ds(base, count)
        return [
            remote(seed_buf.at[block], seed_buf.at[block], 2 * step, partners[step]),
            remote(kv_buf.at[block], kv_buf.at[block], 2 * step + 1, partners[step]),
        ]

    flight = gather(0)
    for copy in flight:
        copy.start()
    sent = list(flight)
    shift_kv = [
        remote(keys, prior_k, 2 * bits, after),
        remote(values, prior_v, 2 * bits + 1, after),
    ]
    shift_state = [
        remote(tail_buf, tail_in, 2 * bits + 2, after),
        remote(state_buf, prior_state, 2 * bits + 3, after),
    ]

    first = me * rows
    start_col = starts_of_column(lengths[...], first, rows)
    start_row = starts_of_row(lengths[...], first, rows)
    same = (start_col == start_row) & (iota((rows, rows), 1) <= iota((rows, rows), 0))
    step_raw = raw[...]
    step_size = jnp.maximum(step_raw, 0.0) + jnp.log(1.0 + jnp.exp(-jnp.abs(step_raw)))
    pad = jnp.zeros((rows, 128 - heads), F32)
    falling = jnp.concatenate([-rate[...] * step_size, pad], axis=1)
    log_step = jnp.concatenate([jnp.log(step_size), pad], axis=1)
    same_f = same.astype(F32)
    same_b = same_f.astype(BF16)
    high = falling.astype(BF16)
    rest = falling - high.astype(F32)
    middle = rest.astype(BF16)
    low_part = (rest - middle.astype(F32)).astype(BF16)
    level = (
        jnp.dot(same_b, low_part, preferred_element_type=F32)
        + jnp.dot(same_b, middle, preferred_element_type=F32)
        + jnp.dot(same_b, high, preferred_element_type=F32)
    )
    last = level[rows - 1:rows, :]
    closing = start_col == start_col[rows - 1:rows, :]
    lo[...] = level
    lo_t[...] = jnp.transpose(level - log_step)
    weight[...] = jnp.where(closing, jnp.exp(jnp.minimum(last - level, 0.0) + log_step), 0.0)
    tail_buf[...] = jnp.broadcast_to(last, tail_buf.shape)
    for g in range(groups):
        write_t[g] = jnp.transpose(write[:, g * size:(g + 1) * size].astype(F32)).astype(BF16)
    low = iota((rows, 128), 1) < 64

    def state_pair(j, carry):
        lanes = pl.ds(pl.multiple_of(j * 128, 128), 128)
        scaled = x[:, lanes].astype(F32) * pair_of(weight[...], 2 * j, low)
        made = jnp.dot(
            write_t[j // pairs_per_group], scaled.astype(BF16), preferred_element_type=F32
        )
        state_buf[:, lanes] = made.astype(BF16)
        return carry

    lax.fori_loop(0, pairs, state_pair, 0, unroll=2)

    @pl.when(me < readers - 1)
    def _():
        for copy in shift_state + shift_kv:
            copy.start()

    half = rows // 2

    def group_step(g):
        at = slice(g * size, (g + 1) * size)
        inner[...] = nt(read[:, at], write[:, at]) * same_f

        def pair_step(k, carry):
            j = g * pairs_per_group + k
            lanes = pl.ds(pl.multiple_of(j * 128, 128), 128)
            for part in range(2):
                here = slice(part * half, (part + 1) * half)
                seen = (part + 1) * half
                x_seen = x[0:seen, lanes]
                products = []
                for side in range(2):
                    head = 2 * j + side
                    own = column_of(lo[here, :], head)
                    eight = lo_t[pl.ds(pl.multiple_of((j // 4) * 8, 8), 8), 0:seen]
                    chosen = iota((8, seen), 0) == lax.rem(j, 4) * 2 + side
                    other = jnp.sum(jnp.where(chosen, eight, 0.0), axis=0, keepdims=True)
                    mixing = inner[here, 0:seen] * jnp.exp(jnp.minimum(own - other, 80.0))
                    products.append(
                        jnp.dot(mixing.astype(BF16), x_seen, preferred_element_type=F32)
                    )
                low_here = iota((half, 128), 1) < 64
                gain = jnp.where(low_here, skip[2 * j], skip[2 * j + 1])
                y_out[here, lanes] = (
                    jnp.where(low_here, products[0], products[1])
                    + gain * x[here, lanes].astype(F32)
                )
            return carry

        lax.fori_loop(0, pairs_per_group, pair_step, 0)

    for index in range(max(bits, groups)):
        if index < groups:
            group_step(index)
        if index < bits:
            for copy in flight:
                copy.wait_recv()
            if index + 1 < bits:
                flight = gather(index + 1)
                for copy in flight:
                    copy.start()
                sent += flight
    for copy in sent:
        copy.wait_send()
    piece = prompt.shape[0]
    for j in range(readers):
        place = sum(((j >> (bits - 1 - step)) & 1) << step for step in range(bits))
        seed_out[j * piece:(j + 1) * piece, :] = seed_buf[place]
        both = kv_buf[place]
        pk_out[j * few:(j + 1) * few, :] = both[0:few]
        pv_out[j * few:(j + 1) * few, :] = both[few:2 * few]

    @pl.when(me == 0)
    def _():
        tail_in[...] = jnp.zeros_like(tail_in)

    @pl.when(me > 0)
    def _():
        for copy in shift_state + shift_kv:
            copy.wait_recv()

    @pl.when(me < readers - 1)
    def _():
        for copy in shift_state + shift_kv:
            copy.wait_send()

    carried = start_col < (me * rows).astype(F32)
    level = lo[...]
    to_prompt = jnp.exp(level + jnp.where(carried, tail_in[0:1, :], 0.0))
    to_state = jnp.where(carried, jnp.exp(level), 0.0)
    for g in range(groups):
        at = slice(g * per_group, (g + 1) * per_group)
        d_prompt[g] = to_prompt[:, at]
        d_state[g] = to_state[:, at]


def attend_kernel(
    group_size, lengths, q, pk, pv, near_k, near_v, own_k, own_v, out, bias
):
    rows = q.shape[0]
    prompts = pk.shape[0]
    half = rows // 2
    me = lax.axis_index("reader")
    first = me * rows

    @pl.when(pl.program_id(0) == 0)
    def _():
        start_col = starts_of_column(lengths[...], first, rows)
        start_row = starts_of_row(lengths[...], first - rows, 2 * rows)
        allowed = (
            (start_col == start_row)
            & (iota((rows, 2 * rows), 1) - rows <= iota((rows, 2 * rows), 0))
        )
        bias[...] = jnp.where(allowed, 0.0, -jnp.inf)

    k_near = jnp.where(me > 0, near_k[...].astype(F32), 0.0).astype(BF16)
    v_near = jnp.where(me > 0, near_v[...].astype(F32), 0.0).astype(BF16)
    k_all = jnp.concatenate([k_near, own_k[...]], axis=0)
    v_all = jnp.concatenate([v_near, own_v[...]], axis=0)
    scale = 1.0 / math.sqrt(HD)
    for part in range(2):
        here = slice(part * half, (part + 1) * half)
        near = slice(part * half, part * half + 3 * half)
        k_part = jnp.concatenate([pk[...], k_all[near]], axis=0)
        v_part = jnp.concatenate([pv[...], v_all[near]], axis=0)
        for j in range(group_size):
            at = slice(j * HD, (j + 1) * HD)
            scores = nt(q[here, at], k_part)
            scores = jnp.concatenate(
                [scores[:, :prompts], scores[:, prompts:] + bias[here, near]], axis=1
            )
            top = jnp.max(scores, axis=1, keepdims=True)
            weights = jnp.exp((scores - top) * scale)
            total = jnp.sum(weights, axis=1, keepdims=True)
            summed = jnp.dot(weights.astype(BF16), v_part, preferred_element_type=F32)
            out[here, at] = (summed / total).astype(BF16)


def finish_kernel(y, read, seed, state, d_prompt, d_state, gate, gain, out, v_buf):
    me = lax.axis_index("reader")
    rows, width = y.shape
    carried_state = jnp.where(me > 0, state[...].astype(F32), 0.0).astype(BF16)
    low = iota((rows, 128), 1) < 64
    square = jnp.zeros((rows, 128), F32)
    for k in range(width // 128):
        at = slice(k * 128, (k + 1) * 128)
        prompt_part = nt(read[...], seed[at, :])
        state_part = jnp.dot(read[...], carried_state[:, at], preferred_element_type=F32)
        by_prompt = jnp.where(
            low, d_prompt[0, :, 2 * k:2 * k + 1], d_prompt[0, :, 2 * k + 1:2 * k + 2]
        )
        by_state = jnp.where(
            low, d_state[0, :, 2 * k:2 * k + 1], d_state[0, :, 2 * k + 1:2 * k + 2]
        )
        mixed = y[:, at] + by_prompt * prompt_part + by_state * state_part
        u = gate[:, at].astype(F32)
        v = mixed * (u / (1.0 + jnp.exp(-u)))
        v_buf[:, at] = v
        square = square + v * v
    mean = jnp.sum(square, axis=1, keepdims=True) * (1.0 / width)
    factor = lax.rsqrt(mean + 1e-05)
    out[...] = (v_buf[...] * factor * gain[...]).astype(BF16)


def local(
    readers,
    answer_lengths, mixer_input, gate_input, state_write, state_read, step_raw, decay_rate,
    skip_gain, norm_gain, prompt_state, queries, answer_keys, answer_values, prompt_keys,
    prompt_values,
):
    rows, channels = mixer_input.shape
    heads = decay_rate.shape[0]
    size = prompt_state.shape[1]
    groups = state_write.shape[1] // size
    per_group = heads // groups
    kv_width = answer_keys.shape[1]
    bits = readers.bit_length() - 1
    lengths = answer_lengths.reshape(1, -1)
    few = prompt_keys.shape[0]
    prompts = readers * few
    piece = prompt_state.shape[0]
    vmem = pl.BlockSpec(memory_space=pltpu.VMEM)
    hbm = pl.BlockSpec(memory_space=pl.ANY)
    smem = pl.BlockSpec(memory_space=pltpu.SMEM)
    shape = jax.ShapeDtypeStruct
    y, seed, pk, pv, d_prompt, d_state, prior_k, prior_v, prior_state = pl.pallas_call(
        functools.partial(mix_kernel, readers, bits, groups),
        out_shape=(
            shape((rows, channels), F32),
            shape((readers * piece, size), BF16),
            shape((prompts, kv_width), BF16),
            shape((prompts, kv_width), BF16),
            shape((groups, rows, per_group), F32),
            shape((groups, rows, per_group), F32),
            shape((rows, kv_width), BF16),
            shape((rows, kv_width), BF16),
            shape((size, channels), BF16),
        ),
        in_specs=[vmem, vmem, vmem, vmem, vmem, vmem, smem, vmem, vmem, vmem, hbm, hbm],
        out_specs=(vmem, vmem, vmem, vmem, vmem, vmem, hbm, hbm, hbm),
        scratch_shapes=[
            pltpu.VMEM((readers, piece, size), BF16),
            pltpu.VMEM((readers, 2 * few, kv_width), BF16),
            pltpu.VMEM((size, channels), BF16),
            pltpu.VMEM((8, 128), F32),
            pltpu.VMEM((8, 128), F32),
            pltpu.VMEM((rows, 128), F32),
            pltpu.VMEM((128, rows), F32),
            pltpu.VMEM((rows, 128), F32),
            pltpu.VMEM((groups, size, rows), BF16),
            pltpu.VMEM((rows, rows), F32),
            pltpu.SemaphoreType.DMA((2 * bits + 4,)),
            pltpu.SemaphoreType.DMA((2 * bits + 4,)),
        ],
        compiler_params=pltpu.CompilerParams(
            collective_id=0, has_side_effects=True, vmem_limit_bytes=VMEM_LIMIT
        ),
        name="mix",
    )(
        lengths, mixer_input, state_write, state_read, step_raw, decay_rate.reshape(1, -1),
        skip_gain, prompt_state, prompt_keys, prompt_values, answer_keys, answer_values,
    )
    kv_heads = kv_width // HD
    group_size = queries.shape[1] // kv_width
    head_block = pl.BlockSpec((rows, HD), lambda k: (0, k))
    prompt_block = pl.BlockSpec((prompts, HD), lambda k: (0, k))
    q_block = pl.BlockSpec((rows, group_size * HD), lambda k: (0, k))
    attention_out = pl.pallas_call(
        functools.partial(attend_kernel, group_size),
        grid=(kv_heads,),
        out_shape=shape(queries.shape, BF16),
        in_specs=[
            pl.BlockSpec(lengths.shape, lambda k: (0, 0)), q_block, prompt_block, prompt_block,
            head_block, head_block, head_block, head_block,
        ],
        out_specs=q_block,
        scratch_shapes=[pltpu.VMEM((rows, 2 * rows), F32)],
        compiler_params=pltpu.CompilerParams(vmem_limit_bytes=VMEM_LIMIT),
        name="attend",
    )(lengths, queries, pk, pv, prior_k, prior_v, answer_keys, answer_values)
    width = channels // groups
    wide = pl.BlockSpec((rows, width), lambda g: (0, g))
    decay_block = pl.BlockSpec((1, rows, per_group), lambda g: (g, 0, 0))
    mixer_out = pl.pallas_call(
        finish_kernel,
        grid=(groups,),
        out_shape=shape((rows, channels), BF16),
        in_specs=[
            wide, pl.BlockSpec((rows, size), lambda g: (0, g)),
            pl.BlockSpec((width, size), lambda g: (g, 0)),
            pl.BlockSpec((size, width), lambda g: (0, g)),
            decay_block, decay_block, wide, pl.BlockSpec((1, width), lambda g: (0, g)),
        ],
        out_specs=wide,
        scratch_shapes=[pltpu.VMEM((rows, width), F32)],
        compiler_params=pltpu.CompilerParams(vmem_limit_bytes=VMEM_LIMIT),
        name="finish",
    )(
        y, state_read, seed, prior_state, d_prompt, d_state, gate_input,
        norm_gain.reshape(1, -1),
    )
    return (mixer_out, attention_out)


def solution(mesh):
    rows = P(("group", "reader"), None)
    in_specs = (P("group"), rows, rows, rows, rows, rows, P(), P(), P(), rows, rows, rows, rows, rows, rows)
    return jax.shard_map(
        functools.partial(local, mesh.shape["reader"]),
        mesh=mesh, in_specs=in_specs, out_specs=(rows, rows), check_vma=False,
    )
```

profile of v0, /device:TPU:9, one launch (start us, length us, event | category | flops | bytes accessed | tf_op | source)
XLA Modules:
  0.0 66.3 jit_solution(18307607222577309398)
XLA Ops:
  0.6 1.6 %copy.17.raw = f32[256,64]{1,0:T(8,128)} copy(f32[256,64]{0,1:T(8,128)} %param.20) | data formatting | bytes 131072 | tf_op args[5]
  2.2 44.0 %mix.1 = (f32[256,4096]{1,0:T(8,128)}, bf16[4096,128]{1,0:T(8,128)(2,1)}, bf16[128,512]{1,0:T(8,128)(2,1)}, bf16[128,512]{1,0:T(8,128)(2,1)}, f32[4,256,16]{2,1,...) custom-call(s32[1,32]{1,0:T(1,128)} %bitcast.4, ...), custom_call_target="tpu_custom_call" | custom-call | tf_op jit(solution)/shard_map/mix/pallas_call | solution.py:326
  46.2 8.9 %finish.1 = bf16[256,4096]{1,0:T(8,128)(2,1)} custom-call(f32[256,4096]{1,0:T(8,128)} %get-tuple-element.11.y, bf16[256,512]{1,0:T(8,128)(2,1)} %read.3, bf16[4096,128]{1,0:T(8,128)(2,1)} %get-tuple-element.12.seed, bf16[128,4096]{1,0:T(8,128)(2,1)} %get-tuple-element.13.state, f32[4,256,16]{2,1,0:T(8,128)} %get-tuple-element.14.d_prompt, ...), custom_call_target="tpu_custom_call" | custom-call | tf_op jit(solution)/shard_map/finish/pallas_call | solution.py:384
  55.1 11.2 %attend.1 = bf16[256,2048]{1,0:T(8,128)(2,1)} custom-call(s32[1,32]{1,0:T(1,128)} %bitcast.5, bf16[256,2048]{1,0:T(8,128)(2,1)} %q.1, bf16[128,512]{1,0:T(8,128)(2,1)} %get-tuple-element.16.pk, bf16[128,512]{1,0:T(8,128)(2,1)} %get-tuple-element.17.pv, bf16[256,512]{1,0:T(8,128)(2,1)} %get-tuple-element.18.near_k, ...), custom_call_target="tpu_custom_call" | custom-call | tf_op jit(solution)/shard_map/attend/pallas_call | solution.py:368
where the time goes:
time: 66.6 us; the launch traced here: 66.3 us
  Pallas kernels  64.1 us (96%)
  local copies, waits for them, and re-layouts  1.59 us (2%)
    pallas_call x1, Pallas kernels, local(): pl.pallas_call(functools.partial(mix_kernel, readers, bits, groups), out_...  44 us
    pallas_call x1, Pallas kernels, local(): pl.pallas_call(functools.partial(attend_kernel, group_size), grid=(kv_hea...  11.2 us
    pallas_call x1, Pallas kernels, local(): pl.pallas_call(finish_kernel, grid=(groups,), out_shape=shape((rows, chan...  8.85 us
    unnamed x1, local copies, waits for them, and re-layouts  1.59 us

commit v1 on v0

v1 whole, which is shorter than its diff:
```python
import functools
import math

import jax
import jax.numpy as jnp
from jax import lax
from jax.experimental import pallas as pl
from jax.experimental.pallas import tpu as pltpu
from jax.sharding import PartitionSpec as P

HD = 128
F32 = jnp.float32
BF16 = jnp.bfloat16
MESH = pl.DeviceIdType.MESH
VMEM_LIMIT = 60 * 1024 * 1024
LOG2E = math.log2(math.e)


def iota(shape, axis):
    return lax.broadcasted_iota(jnp.int32, shape, axis)


def nt(a, b):
    return lax.dot_general(a, b, (((1,), (1,)), ((), ())), preferred_element_type=F32)


def starts_of_column(lengths_row, first, rows):
    n = lengths_row.shape[1]
    wide = jnp.broadcast_to(lengths_row.astype(F32), (8, n)).astype(BF16)
    ahead = (iota((n, n), 0) < iota((n, n), 1)).astype(F32).astype(BF16)
    starts = jnp.dot(wide, ahead, preferred_element_type=F32)[0:1, :]
    place = (iota((rows, n), 0) + first).astype(F32)
    return jnp.max(jnp.where(starts <= place, starts, -1.0), axis=1, keepdims=True)


def starts_of_row(lengths_row, first, columns):
    n = lengths_row.shape[1]
    wide = jnp.broadcast_to(lengths_row.astype(F32), (8, n)).astype(BF16)
    ahead = (iota((n, n), 1) < iota((n, n), 0)).astype(F32).astype(BF16)
    starts = nt(ahead, wide)[:, 0:1]
    place = (iota((n, columns), 1) + first).astype(F32)
    return jnp.max(jnp.where(starts <= place, starts, -1.0), axis=0, keepdims=True)


def column_of(value, index):
    lanes = iota(value.shape, 1)
    return jnp.sum(jnp.where(lanes == index, value, 0.0), axis=1, keepdims=True)


def halves_of(value):
    high = value.astype(BF16)
    return jnp.concatenate([high, (value - high.astype(F32)).astype(BF16)], axis=1)


def pick_of(j):
    head = lax.rem(iota((256, 128), 0), 128) - (iota((256, 128), 1) >= 64).astype(jnp.int32)
    return jnp.where(head == 2 * j, 1.0, 0.0).astype(BF16)


def mix_kernel(
    readers, bits, groups,
    lengths, x, write, read, raw, rate, skip, prompt, pkeys, pvalues, keys, values,
    gain, gate_in, q_in,
    mixer_out, attention_out,
    seed_buf, kv_buf, state_buf, state_prior, tail_buf, tail_in, lo, lo_t, weight, write_t,
    inner, y_out, gate, q, k_all, v_all, bias, d_prompt, d_state,
    send, recv, local_sem,
):
    rows = x.shape[0]
    heads = raw.shape[0]
    size = write.shape[1] // groups
    pairs = x.shape[1] // 128
    pairs_per_group = pairs // groups
    me = lax.axis_index("reader")
    bring_q = pltpu.make_async_copy(q_in, q, local_sem.at[0])
    bring_gate = pltpu.make_async_copy(gate_in, gate, local_sem.at[1])
    bring_q.start()
    bring_gate.start()
    after = lax.rem(me + 1, readers)
    ahead = lax.rem(me + readers - 1, readers)
    partners = []
    slot = 0
    for step in range(bits):
        unit = 1 << (bits - 1 - step)
        bit = lax.rem(me // unit, 2)
        partners.append(me + unit * (1 - 2 * bit))
        slot = slot + bit * (1 << step)
    barrier = pltpu.get_barrier_semaphore()
    for other in partners + [after, ahead]:
        pl.semaphore_signal(barrier, inc=1, device_id={"reader": other}, device_id_type=MESH)
    seed_buf[slot] = prompt[...].astype(BF16)
    few = pkeys.shape[0]
    kv_buf[slot] = jnp.concatenate([pkeys[...], pvalues[...]], axis=0)
    pl.semaphore_wait(barrier, bits + 2)

    def remote(source, target, index, other):
        return pltpu.make_async_remote_copy(
            src_ref=source, dst_ref=target, send_sem=send.at[index], recv_sem=recv.at[index],
            device_id={"reader": other}, device_id_type=MESH,
        )

    def gather(step):
        count = 1 << step
        base = (slot // count) * count
        block = pl.ds(base, count)
        return [
            remote(seed_buf.at[block], seed_buf.at[block], 2 * step, partners[step]),
            remote(kv_buf.at[block], kv_buf.at[block], 2 * step + 1, partners[step]),
        ]

    flights = [gather(step) for step in range(bits)]
    for copy in flights[0]:
        copy.start()

    def advance(step):
        for copy in flights[step]:
            copy.wait_recv()
        if step + 1 < bits:
            for copy in flights[step + 1]:
                copy.start()

    prompts = readers * few
    landing = pl.ds(prompts, rows)
    shift_kv = [
        remote(keys, k_all.at[landing], 2 * bits, after),
        remote(values, v_all.at[landing], 2 * bits + 1, after),
    ]
    shift_state = [
        remote(tail_buf, tail_in, 2 * bits + 2, after),
        remote(state_buf, state_prior, 2 * bits + 3, after),
    ]

    @pl.when(me < readers - 1)
    def _():
        for copy in shift_kv:
            copy.start()

    def launch_state():
        @pl.when(me < readers - 1)
        def _():
            for copy in shift_state:
                copy.start()

    k_all[prompts + rows:prompts + 2 * rows, :] = keys[...]
    v_all[prompts + rows:prompts + 2 * rows, :] = values[...]

    first = me * rows
    start_col = starts_of_column(lengths[...], first, rows)
    start_row = starts_of_row(lengths[...], first, rows)
    same = (start_col == start_row) & (iota((rows, rows), 1) <= iota((rows, rows), 0))
    step_raw = jnp.transpose(
        jnp.concatenate([raw[...], jnp.zeros((128 - raw.shape[0], rows), F32)], axis=0)
    )
    step_size = jnp.maximum(step_raw, 0.0) + jnp.log(1.0 + jnp.exp(-jnp.abs(step_raw)))
    rates = jnp.concatenate([rate[...], jnp.zeros((1, 128 - heads), F32)], axis=1)
    falling = -(LOG2E * rates) * step_size
    log_step = LOG2E * jnp.log(step_size)
    same_f = same.astype(F32)
    same_b = same_f.astype(BF16)
    high = falling.astype(BF16)
    rest = falling - high.astype(F32)
    middle = rest.astype(BF16)
    low_part = (rest - middle.astype(F32)).astype(BF16)
    level = (
        jnp.dot(same_b, low_part, preferred_element_type=F32)
        + jnp.dot(same_b, middle, preferred_element_type=F32)
        + jnp.dot(same_b, high, preferred_element_type=F32)
    )
    last = level[rows - 1:rows, :]
    closing = start_col == start_col[rows - 1:rows, :]
    lo[...] = level
    lo_t[...] = jnp.transpose(level - log_step)
    weight[...] = halves_of(
        jnp.where(closing, jnp.exp2(jnp.minimum(last - level, 0.0) + log_step), 0.0)
    )
    tail_buf[...] = jnp.broadcast_to(last, tail_buf.shape)
    for g in range(groups):
        write_t[g] = jnp.transpose(write[:, g * size:(g + 1) * size].astype(F32)).astype(BF16)

    def state_pair(j, carry):
        lanes = pl.ds(pl.multiple_of(j * 128, 128), 128)
        spread = jnp.dot(weight[...], pick_of(j), preferred_element_type=F32)
        scaled = x[:, lanes].astype(F32) * spread
        made = jnp.dot(
            write_t[j // pairs_per_group], scaled.astype(BF16), preferred_element_type=F32
        )
        state_buf[:, lanes] = made.astype(BF16)
        return carry

    lax.fori_loop(0, pairs // 2, state_pair, 0, unroll=2)
    advance(0)
    lax.fori_loop(pairs // 2, pairs, state_pair, 0, unroll=2)

    half = rows // 2

    def group_step(g):
        at = slice(g * size, (g + 1) * size)
        inner[...] = nt(read[:, at], write[:, at]) * same_f

        def pair_step(k, carry):
            j = g * pairs_per_group + k
            lanes = pl.ds(pl.multiple_of(j * 128, 128), 128)
            for part in range(2):
                here = slice(part * half, (part + 1) * half)
                seen = (part + 1) * half
                x_seen = x[0:seen, lanes]
                products = []
                for side in range(2):
                    head = 2 * j + side
                    own = column_of(lo[here, :], head)
                    eight = lo_t[pl.ds(pl.multiple_of((j // 4) * 8, 8), 8), 0:seen]
                    chosen = iota((8, seen), 0) == lax.rem(j, 4) * 2 + side
                    other = jnp.sum(jnp.where(chosen, eight, 0.0), axis=0, keepdims=True)
                    mixing = inner[here, 0:seen] * jnp.exp2(jnp.minimum(own - other, 115.0))
                    products.append(
                        jnp.dot(mixing.astype(BF16), x_seen, preferred_element_type=F32)
                    )
                low_here = iota((half, 128), 1) < 64
                gain = jnp.where(low_here, skip[2 * j], skip[2 * j + 1])
                y_out[here, lanes] = (
                    jnp.where(low_here, products[0], products[1])
                    + gain * x[here, lanes].astype(F32)
                )
            return carry

        lax.fori_loop(0, pairs_per_group, pair_step, 0, unroll=2)

    step = 1
    for g in range(groups):
        if g == 1 or g == groups - 1:
            advance(step)
            step += 1
        if g == groups - 1:
            launch_state()
        group_step(g)
    while step < bits:
        advance(step)
        step += 1
    for j in range(readers):
        place = sum(((j >> (bits - 1 - step)) & 1) << step for step in range(bits))
        both = kv_buf[place]
        k_all[j * few:(j + 1) * few, :] = both[0:few]
        v_all[j * few:(j + 1) * few, :] = both[few:2 * few]

    @pl.when(me == 0)
    def _():
        tail_in[...] = jnp.zeros_like(tail_in)
        state_prior[...] = jnp.zeros_like(state_prior)
        k_all[prompts:prompts + rows, :] = jnp.zeros((rows, keys.shape[1]), BF16)
        v_all[prompts:prompts + rows, :] = jnp.zeros((rows, keys.shape[1]), BF16)

    near_row = starts_of_row(lengths[...], first - rows, 2 * rows)
    allowed = (start_col == near_row) & (
        iota((rows, 2 * rows), 1) - rows <= iota((rows, 2 * rows), 0)
    )
    bias[...] = jnp.where(allowed, 0.0, -jnp.inf)
    bring_q.wait()

    @pl.when(me > 0)
    def _():
        for copy in shift_kv:
            copy.wait_recv()

    scale = LOG2E / math.sqrt(HD)
    kv_heads = keys.shape[1] // HD
    group_size = q.shape[1] // keys.shape[1]

    def attend(k, carry):
        kv_lanes = pl.ds(pl.multiple_of(k * HD, HD), HD)
        for part in range(2):
            here = slice(part * half, (part + 1) * half)
            near = slice(part * half, part * half + 3 * half)
            held = slice(prompts + part * half, prompts + part * half + 3 * half)
            for j in range(group_size):
                lanes = pl.ds(pl.multiple_of(k * group_size * HD + j * HD, HD), HD)
                q_part = q[here, lanes]
                far = nt(q_part, k_all[0:prompts, kv_lanes])
                close = nt(q_part, k_all[held, kv_lanes]) + bias[here, near]
                top = jnp.maximum(
                    jnp.max(far, axis=1, keepdims=True), jnp.max(close, axis=1, keepdims=True)
                )
                far = jnp.exp2((far - top) * scale)
                close = jnp.exp2((close - top) * scale)
                total = jnp.sum(far, axis=1, keepdims=True) + jnp.sum(
                    close, axis=1, keepdims=True
                )
                summed = jnp.dot(
                    far.astype(BF16), v_all[0:prompts, kv_lanes], preferred_element_type=F32
                ) + jnp.dot(
                    close.astype(BF16), v_all[held, kv_lanes], preferred_element_type=F32
                )
                attention_out[here, lanes] = (summed / total).astype(BF16)
        return carry

    lax.fori_loop(0, kv_heads, attend, 0)

    bring_gate.wait()

    @pl.when(me > 0)
    def _():
        for copy in shift_state:
            copy.wait_recv()

    carried = start_col < (me * rows).astype(F32)
    level = lo[...]
    d_prompt[...] = halves_of(jnp.exp2(level + jnp.where(carried, tail_in[0:1, :], 0.0)))
    d_state[...] = halves_of(jnp.where(carried, jnp.exp2(level), 0.0))
    width = x.shape[1] // groups
    piece = prompt.shape[0]
    for g in range(groups):
        read_part = read[:, g * size:(g + 1) * size]

        def finish(k, square):
            j = g * pairs_per_group + k
            lanes = pl.ds(pl.multiple_of(j * 128, 128), 128)
            row = j * 128
            owner = row // piece
            parts = []
            for one in range(max(1, 128 // piece)):
                number = owner + one
                place = 0
                for step in range(bits):
                    unit = 1 << (bits - 1 - step)
                    place = place + lax.rem(number // unit, 2) * (1 << step)
                if piece >= 128:
                    offset = pl.multiple_of(lax.rem(row, piece), 128)
                    parts.append(seed_buf[place, pl.ds(offset, 128), :])
                else:
                    parts.append(seed_buf[place])
            seed = parts[0] if len(parts) == 1 else jnp.concatenate(parts, axis=0)
            pick = pick_of(j)
            by_prompt = jnp.dot(d_prompt[...], pick, preferred_element_type=F32)
            by_state = jnp.dot(d_state[...], pick, preferred_element_type=F32)
            mixed = (
                y_out[:, lanes]
                + by_prompt * nt(read_part, seed)
                + by_state
                * jnp.dot(read_part, state_prior[:, lanes], preferred_element_type=F32)
            )
            u = gate[:, lanes].astype(F32)
            v = mixed * (u / (1.0 + jnp.exp(-u)))
            y_out[:, lanes] = v
            return square + v * v

        square = lax.fori_loop(0, pairs_per_group, finish, jnp.zeros((rows, 128), F32), unroll=2)
        mean = jnp.sum(square, axis=1, keepdims=True) * (1.0 / width)
        at = slice(g * width, (g + 1) * width)
        mixer_out[:, at] = (
            y_out[:, at] * lax.rsqrt(mean + 1e-05) * gain[:, at]
        ).astype(BF16)

    for flight in flights:
        for copy in flight:
            copy.wait_send()

    @pl.when(me < readers - 1)
    def _():
        for copy in shift_state + shift_kv:
            copy.wait_send()


def local(
    readers,
    answer_lengths, mixer_input, gate_input, state_write, state_read, step_raw, decay_rate,
    skip_gain, norm_gain, prompt_state, queries, answer_keys, answer_values, prompt_keys,
    prompt_values,
):
    rows, channels = mixer_input.shape
    heads = decay_rate.shape[0]
    size = prompt_state.shape[1]
    groups = state_write.shape[1] // size
    kv_width = answer_keys.shape[1]
    bits = readers.bit_length() - 1
    lengths = answer_lengths.reshape(1, -1)
    few = prompt_keys.shape[0]
    prompts = readers * few
    piece = prompt_state.shape[0]
    vmem = pl.BlockSpec(memory_space=pltpu.VMEM)
    hbm = pl.BlockSpec(memory_space=pl.ANY)
    smem = pl.BlockSpec(memory_space=pltpu.SMEM)
    shape = jax.ShapeDtypeStruct
    mixer_out, attention_out = pl.pallas_call(
        functools.partial(mix_kernel, readers, bits, groups),
        out_shape=(shape((rows, channels), BF16), shape(queries.shape, BF16)),
        in_specs=[
            vmem, vmem, vmem, vmem, vmem, vmem, smem, vmem, vmem, vmem, vmem, vmem,
            vmem, hbm, hbm,
        ],
        out_specs=(vmem, vmem),
        scratch_shapes=[
            pltpu.VMEM((readers, piece, size), BF16),
            pltpu.VMEM((readers, 2 * few, kv_width), BF16),
            pltpu.VMEM((size, channels), BF16),
            pltpu.VMEM((size, channels), BF16),
            pltpu.VMEM((8, 128), F32),
            pltpu.VMEM((8, 128), F32),
            pltpu.VMEM((rows, 128), F32),
            pltpu.VMEM((128, rows), F32),
            pltpu.VMEM((rows, 256), BF16),
            pltpu.VMEM((groups, size, rows), BF16),
            pltpu.VMEM((rows, rows), F32),
            pltpu.VMEM((rows, channels), F32),
            pltpu.VMEM((rows, channels), BF16),
            pltpu.VMEM(queries.shape, BF16),
            pltpu.VMEM((prompts + 2 * rows, kv_width), BF16),
            pltpu.VMEM((prompts + 2 * rows, kv_width), BF16),
            pltpu.VMEM((rows, 2 * rows), F32),
            pltpu.VMEM((rows, 256), BF16),
            pltpu.VMEM((rows, 256), BF16),
            pltpu.SemaphoreType.DMA((2 * bits + 4,)),
            pltpu.SemaphoreType.DMA((2 * bits + 4,)),
            pltpu.SemaphoreType.DMA((2,)),
        ],
        compiler_params=pltpu.CompilerParams(
            collective_id=0, has_side_effects=True, vmem_limit_bytes=VMEM_LIMIT
        ),
        name="mix",
    )(
        lengths, mixer_input, state_write, state_read, step_raw.T, decay_rate.reshape(1, -1),
        skip_gain, prompt_state, prompt_keys, prompt_values, answer_keys, answer_values,
        norm_gain.reshape(1, -1), gate_input, queries,
    )
    return (mixer_out, attention_out)


def solution(mesh):
    rows = P(("group", "reader"), None)
    in_specs = (P("group"), rows, rows, rows, rows, rows, P(), P(), P(), rows, rows, rows, rows, rows, rows)
    return jax.shard_map(
        functools.partial(local, mesh.shape["reader"]),
        mesh=mesh, in_specs=in_specs, out_specs=(rows, rows), check_vma=False,
    )
```

time: 66.6 us -> 63.3 us (0.950)
  Pallas kernels: 64.1 us -> 58.3 us
  local copies, waits for them, and re-layouts: 1.59 us -> 4.19 us
    pallas_call x2 -> x0, Pallas kernels: 20.1 us -> none  [the longest x1 11.2 us: local(): pl.pallas_call(functools.partial(attend_kernel, group_size), grid=(kv_hea...]
    pallas_call x1, Pallas kernels: 44 us -> 58.3 us  [local(): pl.pallas_call(functools.partial(mix_kernel, readers, bits, groups), out_...]
    unnamed x1 -> x4, local copies, waits for them, and re-layouts: 1.59 us -> 4.19 us
where the time goes in v1:
time: 63.3 us; the launch traced here: 63.1 us
  Pallas kernels  58.3 us (92%)
  local copies, waits for them, and re-layouts  4.19 us (7%)
  between operations  0.65 us (1%)
    pallas_call x1, Pallas kernels, local(): pl.pallas_call(functools.partial(mix_kernel, readers, bits, groups), out_...  58.3 us
    unnamed x4, local copies, waits for them, and re-layouts  4.19 us

profile of v1, /device:TPU:9, one launch (start us, length us, event | category | flops | bytes accessed | tf_op | source)
XLA Modules:
  0.0 63.1 jit_solution(16473842145831150165)
XLA Ops:
  0.6 58.3 %mix.1 = (bf16[256,4096]{1,0:T(8,128)(2,1)}, bf16[256,2048]{1,0:T(8,128)(2,1)}) custom-call(s32[1,32]{1,0:T(1,128)} %bitcast.6, bf16[256,4096]{1,0:T(8,128)(2,1)} %x.1, bf16[256,512]{1,0:T(8,128)(2,1)} %write.1, bf16[256,512]{1,0:T(8,128)(2,1)} %read.1, f32[64,256]{1,0:T(8,128)} %bitcast.4, f32[1,64]{1,0:T(1,128)} %bitcast.7, f32[64]{0:T(128)} %skip.1, ...), custom_call_target="tpu_custom_call" | custom-call | tf_op jit(solution)/shard_map/mix/pallas_call | solution.py:382
  58.9 0.0 copy-start
  58.9 3.2 %copy.19 = bf16[256,4096]{1,0:T(8,128)(2,1)} copy(bf16[256,4096]{1,0:T(8,128)(2,1)} %get-tuple-element.4) | data formatting | bytes 4194304
  62.2 0.0 copy-done
  62.2 1.0 %copy.20 = bf16[256,2048]{1,0:T(8,128)(2,1)} copy(bf16[256,2048]{1,0:T(8,128)(2,1)S(1)} %copy-done) | data formatting | bytes 2097152
Async XLA Ops:
  58.9 3.2 %copy-start = (bf16[256,2048]{1,0:T(8,128)(2,1)S(1)}, bf16[256,2048]{1,0:T(8,128)(2,1)}, u32[]{:S(2)}) copy-start(bf16[256,2048]{1,0:T(8,128)(2,1)} %get-tuple-element.5) | copy-start | bytes 3145732
